TPU v7x, 256 devices: a whole 4x4x8 slice. The times are simulated.
256 devices in a mesh: row: 8 (over y_lo, x), col: 16 (over z, y_hi), lag: 2 (over core).
Axes of the slice: x: 4, y: 4 (y_hi: 2, y_lo: 2; y = y_hi * 2 + y_lo), z: 8, core: 2. Of those that a mesh axis runs over, the one named last changes fastest.
Arguments:
- history: bfloat16 [8, 16, 128, 4096], P('lag', 'col', None, 'row'), may hold values from -6 to 6
- kernel_tiles: bfloat16 [8, 16, 8, 12, 256, 256], P('row', 'col', 'lag'), may hold values from -0.046875 to 0.046875
- tile_rows: int32 [8, 16, 8, 12], P('row', 'col', 'lag'), may hold values from 0 to 31
- tile_cols: int32 [8, 16, 8, 12], P('row', 'col', 'lag'), may hold values from 0 to 15
- tile_count: int32 [8, 16, 8], P('row', 'col', 'lag'), may hold values from 3 to 12, as said below
- base_stress: float32 [128, 65536], P(None, ('row', 'col', 'lag')), may hold values from -6 to 6
- prev_rate: float32 [128, 65536], P(None, ('row', 'col', 'lag')), may hold values from -6 to 6
- direct_effect: float32 [128, 65536], P(None, ('row', 'col', 'lag')), may hold values from 0.5 to 2
- state_var: float32 [128, 65536], P(None, ('row', 'col', 'lag')), may hold values from -2 to 2
Outputs:
- stress_change: float32 [128, 65536], P(None, ('row', 'col', 'lag'))
- new_rate: float32 [128, 65536], P(None, ('row', 'col', 'lag'))
Inputs may be any that keep to these rules, and one draw needn't show every extreme that they name: `tile_count`: every draw has some device and lag with all 12 slots live.
All inputs are finite; a program needn't handle non-finite values.
Results may differ from a plain program's by a relative error of at most 0.0003.
Values may be sent and summed in bfloat16 or wider, within the bound.
A program may use at most 64 MiB of HBM per device.

v0:
```python
import jax
import jax.numpy as jnp
from jax import lax
from jax.sharding import PartitionSpec as P

NEWTON = 4


def inverse_sinh(value):
    magnitude = jnp.abs(value)
    return jnp.sign(value) * jnp.log(magnitude + jnp.sqrt(1.0 + magnitude * magnitude))


def local(
    history,
    kernel_tiles,
    tile_rows,
    tile_cols,
    tile_count,
    base_stress,
    prev_rate,
    direct_effect,
    state_var,
):
    gathered = lax.all_gather(history, "row", axis=3, tiled=True)
    lag_local = gathered.shape[0]
    sims_count = gathered.shape[2]
    tile_side = kernel_tiles.shape[4]
    slots = kernel_tiles.shape[3]
    col_blocks = gathered.shape[3] // tile_side
    blocks = gathered.reshape(lag_local, sims_count, col_blocks, tile_side)
    choose = jax.nn.one_hot(tile_cols[0, 0], col_blocks, dtype=jnp.bfloat16)
    picked = jnp.einsum(
        "lkb,lsbj->lksj", choose, blocks, preferred_element_type=jnp.float32
    ).astype(jnp.bfloat16)
    contrib = jnp.einsum(
        "lksj,lkij->slki", picked, kernel_tiles[0, 0], preferred_element_type=jnp.float32
    )
    rec_local = base_stress.shape[1] * lax.axis_size(("col", "lag"))
    row_blocks = rec_local // tile_side
    alive_mask = (jnp.arange(slots)[None, :] < tile_count[0, 0][:, None]).astype(jnp.float32)
    masked = (contrib * alive_mask[None, :, :, None]).reshape(
        sims_count, lag_local * slots, tile_side
    )
    targets = tile_rows[0, 0].reshape(lag_local * slots)
    placed = (
        jnp.zeros((sims_count, row_blocks, tile_side), jnp.float32).at[:, targets, :].add(masked)
    )
    partial_stress = placed.reshape(sims_count, rec_local)
    stress_change = lax.psum_scatter(
        partial_stress, ("col", "lag"), scatter_dimension=1, tiled=True
    )
    driving = base_stress + stress_change
    factor = jnp.exp(state_var) / 2.0
    velocity = prev_rate
    for step in range(NEWTON):
        scaled = velocity * factor
        misfit = direct_effect * inverse_sinh(scaled) + 0.5 * velocity - driving
        slope = direct_effect * factor / jnp.sqrt(1.0 + scaled * scaled) + 0.5
        velocity = velocity - misfit / slope
    return (stress_change, velocity)


def solution(mesh):
    return jax.shard_map(
        local,
        mesh=mesh,
        in_specs=(
            P("lag", "col", None, "row"),
            P("row", "col", "lag", None, None, None),
            P("row", "col", "lag", None),
            P("row", "col", "lag", None),
            P("row", "col", "lag"),
            P(None, ("row", "col", "lag")),
            P(None, ("row", "col", "lag")),
            P(None, ("row", "col", "lag")),
            P(None, ("row", "col", "lag")),
        ),
        out_specs=(P(None, ("row", "col", "lag")), P(None, ("row", "col", "lag"))),
        check_vma=False,
    )
```

profile of v0, /device:TPU:2, one launch (start us, length us, event | category | flops | bytes accessed | tf_op | source)
XLA Modules:
  0.0 238.6 jit_solution(9200661468580223937)
XLA Ops:
  7.2 0.0 all-gather.2.cloned.1.call-start
  7.2 0.7 all-gather.2.cloned.1.call-update
  7.9 0.0 reduce-scatter.2.cloned.1.call-start
  7.9 0.8 reshape_squeeze.3
  8.7 0.7 fusion.12
  9.4 56.3 %all-gather.2.cloned.1.call-done = bf16[4,1,128,4096]{3,2,1,0:T(8,128)(2,1)} async-done(((bf16[4,1,128,512]{3,2,1,0:T(8,128)(2,1)}), bf16[4,1,128,4096]{3,2,1,0:T(8,128)(2,1)}) %all-gather.2.cloned.1.call-update) | async-done | bytes 4194320 | tf_op jit(solution)/shard_map/all_gather | solution.py:25
  65.7 0.0 copy-start.4
  65.7 0.0 slice-start
  65.7 3.8 %copy.26 = bf16[64,8,16,256]{3,2,1,0:T(8,128)(2,1)S(1)} copy(bf16[64,8,16,256]{3,1,2,0:T(8,128)(2,1)} %bitcast.34) | data formatting | bytes 8388608
  69.5 0.0 slice-start.1
  69.5 0.0 copy-done.4
  69.5 1.3 fusion.2
  70.8 0.0 slice-done
  70.8 0.3 slice-done.1
  71.1 4.8 %broadcast_multiply_fusion = f32[4,12,128,256]{3,2,1,0:T(8,128)} fusion(f32[4,12]{1,0:T(4,128)S(1)} %fusion.12, bf16[1,1,4,12,256,256]{5,4,3,2,1,0:T(8,128)(2,1)S(1)} %bitcast.33, bf16[4,12,128,256]{3,1,2,0:T(8,128)(2,1)S(1)} %fusion.2), kind=kOutput, calls=%fused_computation.6 | convolution fusion | flops 806879232 | bytes 15728832 | tf_op jit(solution)/shard_map/lksj,lkij->slki/dot_general | solution.py:36
  75.9 2.5 %broadcast_in_dim.4 = f32[128,32,256]{2,0,1:T(8,128)} broadcast(f32[]{:T(128)} %constant.5.clone.1), dimensions={} | broadcast | bytes 4194308 | tf_op jit(solution)/shard_map/broadcast_in_dim | solution.py:47
  78.4 14.6 %scatter_fusion = f32[128,32,256]{2,0,1:T(8,128)} fusion(f32[128,32,256]{2,0,1:T(8,128)} %broadcast_in_dim.4, s32[48]{0:T(128)S(1)} %fusion.13, f32[48,128,256]{2,1,0:T(8,128)} %bitcast.29), kind=kCustom, calls=%fused_computation | custom fusion | flops 1572864 | bytes 18874560 | tf_op jit(solution)/shard_map/scatter-add | solution.py:47
  93.1 5.6 %copy.11 = f32[128,32,256]{0,2,1:T(8,128)} copy(f32[128,32,256]{2,0,1:T(8,128)} %scatter_fusion) | data formatting | bytes 8388608 | tf_op jit(solution)/shard_map/scatter-add | solution.py:47
  98.7 0.0 copy-start
  98.7 0.0 copy-start.1
  98.7 0.0 copy-start.2
  98.7 0.0 copy-start.3
  98.7 0.0 reduce-scatter.2.cloned.1.call-update
  98.7 0.9 copy-done
  99.6 0.1 copy.12
  99.7 0.0 copy-done.1
  99.7 0.1 copy.14
  99.8 0.0 copy-done.2
  99.8 0.1 copy.16
  99.9 0.0 copy-done.3
  99.9 0.1 copy.18
  100.0 127.8 %reduce-scatter.2.cloned.1.call-done = f32[128,256]{0,1:T(8,128)} async-done(((f32[128,8192]{0,1:T(8,128)}), f32[128,256]{0,1:T(8,128)}) %reduce-scatter.2.cloned.1.call-update) | async-done | bytes 131088 | tf_op jit(solution)/shard_map/reduce_scatter | solution.py:50
  227.8 1.5 divide_subtract_fusion
  229.3 0.8 copy.23
  230.1 1.7 copy.22
  (2 shorter events, 0.0 us)
Async XLA Ops:
  7.2 58.6 %all-gather.2.cloned.1.call-start = ((), (), s32[]{:S(2)}) async-start(), calls=%async_computation.1 | async-start | bytes 4718592 | tf_op jit(solution)/shard_map/all_gather | solution.py:25
  7.9 219.9 %reduce-scatter.2.cloned.1.call-start = ((), (), s32[]{:S(2)}) async-start(), calls=%async_computation.2 | async-start | bytes 4325376 | tf_op jit(solution)/shard_map/reduce_scatter | solution.py:50
  65.7 3.8 %copy-start.4 = (s32[1,1,4,12]{3,2,1,0:T(4,128)S(1)}, s32[1,1,4,12]{3,2,1,0:T(4,128)}, u32[]{:S(2)}) copy-start(s32[1,1,4,12]{3,2,1,0:T(4,128)} %param.12) | copy-start | bytes 580
  65.7 5.1 %slice-start = ((s8[6291456]{0:T(1024)(128)(4,1)}), s8[4194304]{0:T(1024)(128)(4,1)S(1)}, s32[]{:S(2)}) async-start(s8[6291456]{0:T(1024)(128)(4,1)} %bitcast.32), calls=%async_computation.3 | async-start | bytes 8388608
  69.5 1.6 slice-start.1
  98.7 0.9 copy-start
  98.7 1.0 copy-start.1
  98.7 1.1 copy-start.2
  98.7 1.2 copy-start.3
Sparse Core Ops, SparseCore 0:
  9.8 55.8 all-gather.1
  98.8 128.9 reduce-scatter.1
where the time goes:
time: 239 us
  waiting for transfers between devices  185 us (77%)
  other arithmetic  16.9 us (7%)
  local copies, waits for them, and re-layouts  16.5 us (7%)
  between operations  14.1 us (6%)
  matrix products  6.13 us (3%)
    reduce_scatter x1, waiting for transfers between devices, local(): lax.psum_scatter(partial_stress, ('col', 'lag'), scatter_dimension=1, til...  128 us
    all_gather x1, waiting for transfers between devices, local(): gathered = lax.all_gather(history, 'row', axis=3, tiled=True)  56.3 us
    scatter-add x1, other arithmetic, local(): jnp.zeros((sims_count, row_blocks, tile_side), jnp.float32)  14.6 us
    unnamed x21, local copies, waits for them, and re-layouts  7.69 us
    scatter-add x1, local copies, waits for them, and re-layouts, local(): jnp.zeros((sims_count, row_blocks, tile_side), jnp.float32)  5.58 us
    dot_general x1, matrix products, local(): jnp.einsum('lksj,lkij->slki', picked, kernel_tiles[0, 0], preferred_eleme...  4.84 us
  transfers between devices with their start and end apart: 2, of which 2 were waited for; matrix products, arithmetic and copies ran while one was open for 1% of the time, Pallas kernels for 0%

commit v1 on v0

--- a/solution.py
+++ b/solution.py
@@ -22,7 +22,9 @@
     direct_effect,
     state_var,
 ):
-    gathered = lax.all_gather(history, "row", axis=3, tiled=True)
+    gathered = jnp.concatenate(
+        lax.all_to_all(jnp.stack([history] * lax.axis_size("row")), "row", 0, 0), axis=3
+    )
     lag_local = gathered.shape[0]
     sims_count = gathered.shape[2]
     tile_side = kernel_tiles.shape[4]

time: 239 us -> 264 us (1.10)
  local copies, waits for them, and re-layouts: 16.5 us -> 29 us
  starting transfers between devices: 0.08 us -> 6.83 us
  waiting for transfers between devices: 185 us -> 189 us
    all_gather x1 -> x0, waiting for transfers between devices: 56.3 us -> none  [local(): gathered = lax.all_gather(history, 'row', axis=3, tiled=True)]
    all_to_all x0 -> x1, waiting for transfers between devices: none -> 55.7 us  [local(): lax.all_to_all(jnp.stack([history] * lax.axis_size('row')), 'row', 0, 0)]
    another operation x0 -> x3, local copies, waits for them, and re-layouts: none -> 12.1 us  [the longest x1 7.87 us: local(): blocks = gathered.reshape(lag_local, sims_count, col_blocks, tile_side)]
    all_to_all x0 -> x1, starting transfers between devices: none -> 6.82 us  [local(): lax.all_to_all(jnp.stack([history] * lax.axis_size('row')), 'row', 0, 0)]
    reduce_scatter x1, waiting for transfers between devices: 128 us -> 133 us  [local(): lax.psum_scatter(partial_stress, ('col', 'lag'), scatter_dimension=1, til...]
    all_to_all x0 -> x1, local copies, waits for them, and re-layouts: none -> 4.61 us  [local(): lax.all_to_all(jnp.stack([history] * lax.axis_size('row')), 'row', 0, 0)]
    unnamed x21 -> x24, local copies, waits for them, and re-layouts: 7.69 us -> 4.14 us
  transfers between devices with their start and end apart: 2 -> 2, of which waited for: 2 -> 2; matrix products, arithmetic and copies ran while one was open for 1% -> 0% of each run, Pallas kernels for 0% -> 0%
where the time goes in v1:
time: 264 us
  waiting for transfers between devices  189 us (72%)
  local copies, waits for them, and re-layouts  29 us (11%)
  other arithmetic  16.3 us (6%)
  between operations  14.1 us (5%)
  matrix products  8.46 us (3%)
  starting transfers between devices  6.83 us (3%)
    reduce_scatter x1, waiting for transfers between devices, local(): lax.psum_scatter(partial_stress, ('col', 'lag'), scatter_dimension=1, til...  133 us
    all_to_all x1, waiting for transfers between devices, local(): lax.all_to_all(jnp.stack([history] * lax.axis_size('row')), 'row', 0, 0)  55.7 us
    scatter-add x1, other arithmetic, local(): jnp.zeros((sims_count, row_blocks, tile_side), jnp.float32)  14.7 us
    another operation x1, local copies, waits for them, and re-layouts, local(): blocks = gathered.reshape(lag_local, sims_count, col_blocks, tile_side)  7.87 us
    all_to_all x1, starting transfers between devices, local(): lax.all_to_all(jnp.stack([history] * lax.axis_size('row')), 'row', 0, 0)  6.82 us
    scatter-add x1, local copies, waits for them, and re-layouts, local(): jnp.zeros((sims_count, row_blocks, tile_side), jnp.float32)  5.59 us
  transfers between devices with their start and end apart: 2, of which 2 were waited for; matrix products, arithmetic and copies ran while one was open for 0% of the time, Pallas kernels for 0%

profile of v1, /device:TPU:2, one launch (start us, length us, event | category | flops | bytes accessed | tf_op | source)
XLA Modules:
  0.0 263.9 jit_solution(7377654217200679762)
XLA Ops:
  7.2 1.3 copy.25
  8.5 2.9 %stack.2 = bf16[8,4,1,128,512]{3,4,1,2,0:T(8,128)(2,1)} broadcast(bf16[4,128,512]{1,2,0:T(8,128)(2,1)S(1)} %copy.25), dimensions={1,3,4} | broadcast | bytes 4718592 | tf_op jit(solution)/shard_map/stack | solution.py:26
  11.4 0.0 copy-start.5
  11.4 0.0 copy-start.6
  11.4 6.8 %all-to-all-start = ((bf16[8,4,1,128,512]{3,4,1,2,0:T(8,128)(2,1)}), bf16[8,4,1,128,512]{3,4,1,2,0:T(8,128)(2,1)}, u32[]{:S(2)}, u32[]{:S(2)}) async-start(bf16[8,4,1,128,512]{3,4,1,2,0:T(8,128)(2,1)} %stack.2), calls=%async_computation | async-start | bytes 8388608 | tf_op jit(solution)/shard_map/all_to_all | solution.py:26
  18.2 0.0 reduce-scatter.2.cloned.1.call-start
  18.2 0.0 copy-done.5
  18.2 0.1 reshape_squeeze.3
  18.3 0.0 copy-done.6
  18.3 0.1 fusion.13
  18.4 55.7 %all-to-all-done = bf16[8,4,1,128,512]{3,4,1,2,0:T(8,128)(2,1)} async-done(((bf16[8,4,1,128,512]{3,4,1,2,0:T(8,128)(2,1)}), bf16[8,4,1,128,512]{3,4,1,2,0:T(8,128)(2,1)}, u32[]{:S(2)}, u32[]{:S(2)}) %all-to-all-start) | async-done | bytes 4194336 | tf_op jit(solution)/shard_map/all_to_all | solution.py:26
  74.1 4.6 %copy.26 = bf16[8,4,1,128,512]{3,4,0,1,2:T(8,128)(2,1)} copy(bf16[8,4,1,128,512]{3,4,1,2,0:T(8,128)(2,1)} %all-to-all-done) | data formatting | bytes 8388608 | tf_op jit(solution)/shard_map/all_to_all | solution.py:26
  78.7 0.0 copy-start.4
  78.7 7.9 %copy.27 = bf16[4,128,16,256]{3,2,1,0:T(8,128)(2,1)} copy(bf16[4,128,16,256]{1,3,2,0:T(8,128)(2,1)} %bitcast.27) | data formatting | bytes 8388608 | tf_op jit(solution)/shard_map/reshape;reshape | solution.py:33
  86.6 0.0 slice-start
  86.6 0.0 copy-done.4
  86.6 0.0 slice-start.1
  86.6 3.6 %convolution_convert_fusion = bf16[4,12,128,256]{3,1,2,0:T(8,128)(2,1)S(1)} fusion(bf16[4,128,16,256]{3,2,1,0:T(8,128)(2,1)} %copy.27, s32[4,12]{1,0:T(4,128)S(1)} %bitcast.31), kind=kOutput, calls=%fused_computation.5 | convolution fusion | flops 51905280 | bytes 7340224 | tf_op jit(solution)/shard_map/lkb,lsbj->lksj/dot_general | solution.py:35
  90.2 0.0 slice-done
  90.2 0.5 slice-done.1
  90.7 4.8 %broadcast_multiply_fusion = f32[4,12,128,256]{3,2,1,0:T(8,128)} fusion(f32[4,12]{1,0:T(4,128)S(1)} %fusion.13, bf16[1,1,4,12,256,256]{5,4,3,2,1,0:T(8,128)(2,1)S(1)} %bitcast.29, bf16[4,12,128,256]{3,1,2,0:T(8,128)(2,1)S(1)} %convolution_convert_fusion), kind=kOutput, calls=%fused_computation.4 | convolution fusion | flops 806879232 | bytes 15728832 | tf_op jit(solution)/shard_map/lksj,lkij->slki/dot_general | solution.py:38
  95.5 2.5 broadcast_in_dim.4
  98.0 14.7 %scatter_fusion = f32[128,32,256]{2,0,1:T(8,128)} fusion(f32[128,32,256]{2,0,1:T(8,128)} %broadcast_in_dim.4, s32[48]{0:T(128)S(1)} %fusion.14, f32[48,128,256]{2,1,0:T(8,128)} %bitcast.25), kind=kCustom, calls=%fused_computation | custom fusion | flops 1572864 | bytes 18874560 | tf_op jit(solution)/shard_map/scatter-add | solution.py:49
  112.8 5.6 %copy.29 = f32[128,32,256]{0,2,1:T(8,128)} copy(f32[128,32,256]{2,0,1:T(8,128)} %scatter_fusion) | data formatting | bytes 8388608 | tf_op jit(solution)/shard_map/scatter-add | solution.py:49
  118.3 0.0 copy-start
  118.3 0.0 copy-start.1
  118.3 0.0 copy-start.2
  118.4 0.0 copy-start.3
  118.4 0.0 reduce-scatter.2.cloned.1.call-update
  118.4 0.9 copy-done
  119.2 0.1 copy.30
  119.3 0.0 copy-done.1
  119.4 0.1 copy.32
  119.4 0.0 copy-done.2
  119.5 0.1 copy.34
  119.6 0.0 copy-done.3
  119.6 0.1 copy.36
  119.7 133.5 %reduce-scatter.2.cloned.1.call-done = f32[128,256]{0,1:T(8,128)} async-done(((f32[128,8192]{0,1:T(8,128)}), f32[128,256]{0,1:T(8,128)}) %reduce-scatter.2.cloned.1.call-update) | async-done | bytes 131088 | tf_op jit(solution)/shard_map/reduce_scatter | solution.py:52
  253.1 1.5 divide_subtract_fusion
  254.6 0.8 copy.41
  255.4 1.7 copy.40
  (2 shorter events, 0.0 us)
Async XLA Ops:
  11.4 6.8 %copy-start.5 = (s32[1,1,4,12]{3,2,1,0:T(4,128)S(1)}, s32[1,1,4,12]{3,2,1,0:T(4,128)}, u32[]{:S(2)}) copy-start(s32[1,1,4,12]{3,2,1,0:T(4,128)} %param.11) | copy-start | bytes 580
  11.4 6.9 %copy-start.6 = (s32[1,1,4]{2,1,0:T(1,128)S(1)}, s32[1,1,4]{2,1,0:T(1,128)}, u32[]{:S(2)}) copy-start(s32[1,1,4]{2,1,0:T(1,128)} %param.13) | copy-start | bytes 52
  11.4 62.7 %all-to-all-start = ((bf16[8,4,1,128,512]{3,4,1,2,0:T(8,128)(2,1)}), bf16[8,4,1,128,512]{3,4,1,2,0:T(8,128)(2,1)}, u32[]{:S(2)}, u32[]{:S(2)}) async-start(bf16[8,4,1,128,512]{3,4,1,2,0:T(8,128)(2,1)} %stack.2), calls=%async_computation | async-start | bytes 8388608 | tf_op jit(solution)/shard_map/all_to_all | solution.py:26
  18.2 234.9 %reduce-scatter.2.cloned.1.call-start = ((), (), s32[]{:S(2)}) async-start(), calls=%async_computation.2 | async-start | bytes 4325376 | tf_op jit(solution)/shard_map/reduce_scatter | solution.py:52
  78.7 7.9 %copy-start.4 = (s32[1,1,4,12]{3,2,1,0:T(4,128)S(1)}, s32[1,1,4,12]{3,2,1,0:T(4,128)}, u32[]{:S(2)}) copy-start(s32[1,1,4,12]{3,2,1,0:T(4,128)} %param.12) | copy-start | bytes 580
  86.6 3.6 %slice-start = ((s8[6291456]{0:T(1024)(128)(4,1)}), s8[4194304]{0:T(1024)(128)(4,1)S(1)}, s32[]{:S(2)}) async-start(s8[6291456]{0:T(1024)(128)(4,1)} %bitcast.28), calls=%async_computation.3 | async-start | bytes 8388608
  86.6 4.1 %slice-start.1 = ((s8[6291456]{0:T(1024)(128)(4,1)}), s8[2097152]{0:T(1024)(128)(4,1)S(1)}, s32[]{:S(2)}) async-start(s8[6291456]{0:T(1024)(128)(4,1)} %bitcast.28), calls=%async_computation.4 | async-start | bytes 4194304
  118.3 0.9 copy-start
  118.3 1.0 copy-start.1
  118.3 1.1 copy-start.2
  118.4 1.2 copy-start.3
Sparse Core Ops, SparseCore 0:
  118.5 134.5 reduce-scatter.1
